TPU v7x, 128 devices: a whole 4x4x4 slice. The times are simulated.
128 devices in a mesh: gx: 8 (over x, core), gy: 16 (over z, y).
Axes of the slice: x: 4, y: 4, z: 4, core: 2. Of those that a mesh axis runs over, the one named last changes fastest.
Arguments:
- parent_fields: float32 [5, 4, 384, 6144], P(None, None, 'gx', 'gy'), may hold values from -6 to 6
- parent_velocity: float32 [2, 4, 384, 6144], P(None, None, 'gx', 'gy'), may hold values from -0.3 to 0.3
- parent_mixing: float32 [4, 384, 6144], P(None, 'gx', 'gy'), may hold values from 0.01 to 0.1
- nest_fields: float32 [5, 4, 384, 6144], P(None, None, 'gx', 'gy'), may hold values from -6 to 6
- nest_velocity: float32 [2, 4, 384, 6144], P(None, None, 'gx', 'gy'), may hold values from -0.3 to 0.3
- nest_mixing: float32 [4, 384, 6144], P(None, 'gx', 'gy'), may hold values from 0.01 to 0.1
- nest_anchor: int32 [2], replicated, may hold values from 1 to 3327, as said below
Outputs:
- parent_result: float32 [5, 4, 384, 6144], P(None, None, 'gx', 'gy')
- nest_result: float32 [5, 4, 384, 6144], P(None, None, 'gx', 'gy')
Inputs may be any that keep to these rules, and one draw needn't show every extreme that they name: `nest_anchor`: the row anchor is 1 to 254; the column anchor is 3073 to 3327, so the nest with a rim of one parent cell lies inside the parent grid.
All inputs are finite; a program needn't handle non-finite values.
Results may differ from a plain program's by a relative error of at most 0.00002.
Values sent between devices are 32-bit elements; how exact they have to be, the bound alone decides.
A program may use at most 192 MiB of HBM per device.

v0:
```python
import jax
import jax.numpy as jnp
from jax import lax
from jax.sharding import PartitionSpec as P

SUBSTEPS = 3
third = 1.0 / 3.0
two_thirds = 2.0 / 3.0
nudge_floor = 0.1
relax_width = 4.0


def extended(cells, sides, width):
    for axis, dim in sides:
        count = lax.axis_size(axis)
        ends = count - 1
        head = lax.slice_in_dim(cells, 0, width, axis=dim)
        tail = lax.slice_in_dim(cells, cells.shape[dim] - width, cells.shape[dim], axis=dim)
        cells = jnp.concatenate(
            [
                lax.ppermute(tail, axis, [(i, (i + 1) % count) for i in range(ends)]),
                cells,
                lax.ppermute(head, axis, [((i + 1) % count, i) for i in range(ends)]),
            ],
            axis=dim,
        )
    return cells


def update(values, padded, velocity, mixing):
    western = padded[:, :, :-2, 1:-1]
    eastern = padded[:, :, 2:, 1:-1]
    southern = padded[:, :, 1:-1, :-2]
    northern = padded[:, :, 1:-1, 2:]
    along_rows = velocity[0]
    along_columns = velocity[1]
    upwind = (
        jnp.maximum(along_rows, 0.0) * (values - western)
        + jnp.minimum(along_rows, 0.0) * (eastern - values)
        + jnp.maximum(along_columns, 0.0) * (values - southern)
        + jnp.minimum(along_columns, 0.0) * (northern - values)
    )
    return values - upwind + mixing * (eastern + western + northern + southern - 4.0 * values)


def refine_rows(block):
    lower = block[:, :, :-2]
    centre = block[:, :, 1:-1]
    upper = block[:, :, 2:]
    stacked = jnp.stack(
        (third * lower + two_thirds * centre, centre, two_thirds * centre + third * upper), axis=3
    )
    extent = centre.shape
    return stacked.reshape(extent[0], extent[1], 3 * extent[2], extent[3])


def refine_columns(block):
    lower = block[:, :, :, :-2]
    centre = block[:, :, :, 1:-1]
    upper = block[:, :, :, 2:]
    stacked = jnp.stack(
        (third * lower + two_thirds * centre, centre, two_thirds * centre + third * upper), axis=4
    )
    extent = centre.shape
    return stacked.reshape(extent[0], extent[1], extent[2], 3 * extent[3])


def block_mean(state):
    extent = state.shape
    grouped = state.reshape(extent[0], extent[1], extent[2] // 3, 3, extent[3] // 3, 3)
    return jnp.sum(grouped, axis=(3, 5)) / 9.0


def relax_weight(row_global, column_global, total_rows, total_columns):
    row_distance = jnp.minimum(row_global, total_rows - 1 - row_global)
    column_distance = jnp.minimum(column_global, total_columns - 1 - column_global)
    distance = jnp.minimum(row_distance[:, None], column_distance[None, :]).astype(jnp.float32)
    return nudge_floor + (1.0 - nudge_floor) * jnp.exp(-distance / relax_width)


def take_rows(values, positions, valid):
    picked = jnp.take(values, jnp.clip(positions, 0, values.shape[2] - 1), axis=2)
    return jnp.where(valid[:, None], picked, 0.0)


def take_columns(values, positions, valid):
    picked = jnp.take(values, jnp.clip(positions, 0, values.shape[3] - 1), axis=3)
    return jnp.where(valid, picked, 0.0)


def within(positions, limit):
    return (positions >= 0) & (positions < limit)


def spans(anchor, count, length):
    offsets = (
        jnp.arange(count, dtype=jnp.int32)[:, None] * length
        + jnp.arange(length + 2, dtype=jnp.int32)[None, :]
    )
    return anchor - 1 + offsets.reshape(-1)


def owner_mask(owners, count):
    return (owners[None, :] == jnp.arange(count, dtype=jnp.int32)[:, None]).reshape(-1)


def spread_rows(values, owners, count):
    tiled = jnp.tile(values, (1, 1, count, 1))
    return jnp.where(owner_mask(owners, count)[:, None], tiled, 0.0)


def spread_columns(values, owners, count):
    tiled = jnp.tile(values, (1, 1, 1, count))
    return jnp.where(owner_mask(owners, count), tiled, 0.0)


def per_device(
    parent_fields,
    parent_velocity,
    parent_mixing,
    nest_fields,
    nest_velocity,
    nest_mixing,
    nest_anchor,
):
    row_rank = lax.axis_index("gx")
    column_rank = lax.axis_index("gy")
    row_devices = lax.axis_size("gx")
    column_devices = lax.axis_size("gy")
    fields_count = parent_fields.shape[0]
    levels_count = parent_fields.shape[1]
    parent_rows = parent_fields.shape[2]
    parent_columns = parent_fields.shape[3]
    nest_rows = nest_fields.shape[2]
    nest_columns = nest_fields.shape[3]
    span_rows = nest_rows // 3
    span_columns = nest_columns // 3
    row_anchor = nest_anchor[0]
    column_anchor = nest_anchor[1]
    parent_padded = extended(parent_fields, (("gx", 2), ("gy", 3)), 1)
    parent_next = update(parent_fields, parent_padded, parent_velocity, parent_mixing)
    row_targets = spans(row_anchor, row_devices, span_rows) - row_rank * parent_rows
    column_targets = (
        spans(column_anchor, column_devices, span_columns) - column_rank * parent_columns
    )
    outgoing = take_columns(parent_next, column_targets, within(column_targets, parent_columns))
    incoming = lax.all_to_all(outgoing, "gy", split_axis=3, concat_axis=3, tiled=True)
    partial_block = incoming.reshape(
        fields_count, levels_count, parent_rows, column_devices, span_columns + 2
    ).sum(axis=3)
    outgoing_rows = take_rows(partial_block, row_targets, within(row_targets, parent_rows))
    incoming_rows = lax.all_to_all(outgoing_rows, "gx", split_axis=2, concat_axis=2, tiled=True)
    relay = incoming_rows.reshape(
        fields_count, levels_count, row_devices, span_rows + 2, span_columns + 2
    ).sum(axis=2)
    forcing = refine_columns(refine_rows(relay))
    row_global = row_rank * nest_rows + jnp.arange(nest_rows, dtype=jnp.int32)
    column_global = column_rank * nest_columns + jnp.arange(nest_columns, dtype=jnp.int32)
    weight = relax_weight(
        row_global, column_global, row_devices * nest_rows, column_devices * nest_columns
    )
    state = nest_fields
    for substep in range(SUBSTEPS):
        nest_padded = extended(state, (("gx", 2), ("gy", 3)), 1)
        moved = update(state, nest_padded, nest_velocity, nest_mixing)
        state = moved + weight * (forcing - moved)
    coarse = block_mean(state)
    own_rows = row_anchor + row_rank * span_rows + jnp.arange(span_rows, dtype=jnp.int32)
    own_columns = (
        column_anchor + column_rank * span_columns + jnp.arange(span_columns, dtype=jnp.int32)
    )
    relative_rows = row_rank * parent_rows + jnp.arange(parent_rows, dtype=jnp.int32) - row_anchor
    relative_columns = (
        column_rank * parent_columns + jnp.arange(parent_columns, dtype=jnp.int32) - column_anchor
    )
    rows_valid = within(relative_rows, row_devices * span_rows)
    columns_valid = within(relative_columns, column_devices * span_columns)
    outgoing = spread_columns(coarse, own_columns // parent_columns, column_devices)
    incoming = lax.all_to_all(outgoing, "gy", split_axis=3, concat_axis=3, tiled=True)
    placed = take_columns(incoming, relative_columns, columns_valid)
    outgoing_rows = spread_rows(placed, own_rows // parent_rows, row_devices)
    incoming_rows = lax.all_to_all(outgoing_rows, "gx", split_axis=2, concat_axis=2, tiled=True)
    fed_back = take_rows(incoming_rows, relative_rows, rows_valid)
    covered = rows_valid[:, None] & columns_valid[None, :]
    parent_result = jnp.where(covered, fed_back, parent_next)
    return (parent_result, state)


def solution(mesh):
    placed = (
        P(None, None, "gx", "gy"),
        P(None, None, "gx", "gy"),
        P(None, "gx", "gy"),
        P(None, None, "gx", "gy"),
        P(None, None, "gx", "gy"),
        P(None, "gx", "gy"),
        P(),
    )
    return jax.shard_map(
        per_device,
        mesh=mesh,
        in_specs=placed,
        out_specs=(P(None, None, "gx", "gy"), P(None, None, "gx", "gy")),
        check_vma=False,
    )
```

profile of v0, /device:TPU:1, one launch (start us, length us, event | category | flops | bytes accessed | tf_op | source)
XLA Modules:
  0.0 732.8 jit_solution(10386896655536340189)
XLA Ops:
  1.9 4.5 collective-permute-start.4
  6.4 1.9 collective-permute-start.5
  10.8 2.1 maximum_bitcast_fusion.1
  14.3 3.2 collective-permute-start.6
  23.3 3.4 fusion.34
  26.7 3.1 copy.257
  29.8 32.2 %gather_fusion = f32[2080,5,4,48]{3,2,1,0:T(4,128)} fusion(f32[5,4,48,384]{2,1,3,0:T(4,128)} %copy.257, s32[3072]{0:T(1024)S(1)} %copy-done.19), kind=kCustom, calls=%fused_computation | custom fusion | bytes 15982720 | tf_op jit(solution)/shard_map/jit(_take)/gather | solution.py:87
  62.0 15.2 %fusion.87 = f32[2080,5,4,48]{3,2,1,0:T(4,128)} fusion(f32[2080,5,4,48]{3,2,1,0:T(4,128)} %gather_fusion, pred[2080]{0:T(1024)(128)(4,1)S(1)} %copy-done.21, pred[2080]{0:T(1024)(128)(4,1)S(1)} %copy-done.20), kind=kLoop, calls=%fused_computation.195 | loop fusion | flops 3993600 | bytes 15978560
  77.2 26.0 %reshape.359 = f32[16,1,124800]{2,1,0:T(1,128)} reshape(f32[2080,5,4,48]{3,2,1,0:T(4,128)} %fusion.87) | data formatting | bytes 15974400
  103.2 9.4 %all-to-all-start = ((f32[16,1,124800]{2,1,0:T(1,128)}), f32[16,1,124800]{2,1,0:T(1,128)}, u32[]{:S(2)}, u32[]{:S(2)}) async-start(f32[16,1,124800]{2,1,0:T(1,128)} %reshape.359), calls=%async_computation | async-start | bytes 15974400 | tf_op jit(solution)/shard_map/all_to_all | solution.py:147
  113.7 120.9 %all-to-all-done = f32[16,1,124800]{2,1,0:T(1,128)} async-done(((f32[16,1,124800]{2,1,0:T(1,128)}), f32[16,1,124800]{2,1,0:T(1,128)}, u32[]{:S(2)}, u32[]{:S(2)}) %all-to-all-start) | async-done | bytes 7987232 | tf_op jit(solution)/shard_map/all_to_all | solution.py:147
  235.2 24.6 %reduce.4 = f32[16,124800]{1,0:T(8,128)} reduce(f32[16,1,124800]{2,1,0:T(1,128)} %all-to-all-done, f32[]{:T(128)} %broadcast.601), dimensions={1}, to_apply=%all_to_all.12.reduce_sub_computation | reduce | bytes 15974404 | tf_op jit(solution)/shard_map/all_to_all | solution.py:147
  259.8 28.8 %reshape.360 = f32[2080,5,4,48]{3,2,1,0:T(4,128)} reshape(f32[16,124800]{1,0:T(8,128)} %reduce.4) | data formatting | bytes 15974400
  288.6 11.8 %reduce_sum.27 = f32[5,4,48,130]{2,1,0,3:T(4,128)S(1)} reduce(f32[5,4,48,16,130]{2,1,0,4,3:T(4,128)} %bitcast.60, f32[]{:T(128)} %constant.66.clone.1), dimensions={3}, to_apply=%region_0.1 | reduce | flops 1872000 | bytes 8486404 | tf_op jit(solution)/shard_map/reduce_sum | solution.py:150
  302.0 4.3 gather_fusion.1
  306.3 4.1 select_bitcast_fusion.2
  310.5 4.3 all-to-all-start.1
  316.1 3.5 collective-permute-start
  322.7 24.9 %collective-permute-done = f32[5,4,1,384]{3,1,2,0:T(4,128)S(1)} collective-permute-done((f32[5,4,1,384]{3,1,2,0:T(4,128)S(1)}, f32[5,4,1,384]{3,1,2,0:T(4,128)S(1)}, u32[]{:S(2)}, u32[]{:S(2)}) %collective-permute-start) | collective-permute-done | bytes 30752 | tf_op jit(solution)/shard_map/ppermute | solution.py:21
  347.7 2.0 collective-permute-done.1
  362.3 3.6 copy.262
  365.8 3.5 copy.263
  369.4 3.6 multiply_add_fusion.2
  373.1 3.5 collective-permute-start.8
  378.6 3.2 collective-permute-done.9
  389.9 5.7 multiply_add_fusion.1
  395.7 3.3 collective-permute-start.12
  401.5 2.7 collective-permute-done.13
  406.9 6.1 collective-permute-start.14
  421.4 4.6 multiply_add_fusion
  426.0 61.8 %reshape.322 = f32[5,4,16,3,128,3]{5,4,3,2,1,0:T(8,128)} reshape(f32[5,4,48,384]{3,2,1,0:T(8,128)} %multiply_add_fusion) | data formatting | bytes 2949120 | tf_op jit(solution)/shard_map/reshape | solution.py:70
  487.7 20.5 %reduce_sum.29 = f32[5,4,16,128]{3,2,1,0:T(8,128)S(1)} reduce(f32[5,4,16,3,128,3]{5,4,3,2,1,0:T(8,128)} %reshape.322, f32[]{:T(128)} %constant.66.clone.1), dimensions={3,5}, to_apply=%region_2.3 | reduce | flops 327680 | bytes 1638404 | tf_op jit(solution)/shard_map/reduce_sum | solution.py:71
  508.7 11.5 %bitcast_select_fusion = f32[5,4,16,2048]{2,1,0,3:T(4,128)} fusion(f32[5,4,16,128]{2,1,0,3:T(4,128)S(1)} %copy.286, pred[2048]{0:T(1024)(128)(4,1)S(1)} %fusion.70), kind=kLoop, calls=%fused_computation.5 | loop fusion | flops 655360 | bytes 2787328 | tf_op jit(solution)/shard_map/jit(_where)/select_n | solution.py:114
  520.2 21.1 %reshape.361 = f32[16,1,40960]{2,1,0:T(1,128)} reshape(f32[2048,5,4,16]{3,2,1,0:T(4,128)} %bitcast.61) | data formatting | bytes 5242880
  541.3 8.1 %all-to-all-start.2 = ((f32[16,1,40960]{2,1,0:T(1,128)}), f32[16,1,40960]{2,1,0:T(1,128)S(1)}, u32[]{:S(2)}, u32[]{:S(2)}) async-start(f32[16,1,40960]{2,1,0:T(1,128)} %reshape.361), calls=%async_computation.2 | async-start | bytes 5242880 | tf_op jit(solution)/shard_map/all_to_all | solution.py:179
  552.3 39.2 %all-to-all-done.2 = f32[16,1,40960]{2,1,0:T(1,128)S(1)} async-done(((f32[16,1,40960]{2,1,0:T(1,128)}), f32[16,1,40960]{2,1,0:T(1,128)S(1)}, u32[]{:S(2)}, u32[]{:S(2)}) %all-to-all-start.2) | async-done | bytes 2621472 | tf_op jit(solution)/shard_map/all_to_all | solution.py:179
  591.5 9.1 %reduce.5 = f32[16,40960]{1,0:T(8,128)} reduce(f32[16,1,40960]{2,1,0:T(1,128)S(1)} %all-to-all-done.2, f32[]{:T(128)} %broadcast.601), dimensions={1}, to_apply=%all_to_all.14.reduce_sub_computation | reduce | bytes 5242884 | tf_op jit(solution)/shard_map/all_to_all | solution.py:179
  600.6 25.4 %reshape.362 = f32[2048,5,4,16]{3,2,1,0:T(4,128)} reshape(f32[16,40960]{1,0:T(8,128)} %reduce.5) | data formatting | bytes 5242880
  626.0 17.1 %copy.287 = f32[5,4,16,2048]{2,1,3,0:T(4,128)} copy(f32[5,4,16,2048]{2,1,0,3:T(4,128)} %bitcast.62) | data formatting | bytes 5242880 | tf_op jit(solution)/shard_map/all_to_all | solution.py:179
  643.1 12.3 %gather_fusion.2 = f32[384,5,4,16]{3,2,1,0:T(4,128)} fusion(f32[5,4,16,2048]{2,1,3,0:T(4,128)} %copy.287, s32[1024]{0:T(1024)S(1)} %pad_clamp_fusion.2), kind=kCustom, calls=%fused_computation.2 | custom fusion | bytes 984576 | tf_op jit(solution)/shard_map/jit(_take)/gather | solution.py:87
  655.4 5.9 select_bitcast_fusion.1
  661.3 3.4 copy.288
  664.7 2.9 bitcast_select_fusion.1
  667.6 5.3 all-to-all-start.3
  676.1 42.9 %all-to-all-done.3 = f32[5,4,128,384]{3,1,0,2:T(4,128)} async-done(((f32[5,4,128,384]{3,1,0,2:T(4,128)}), f32[5,4,128,384]{3,1,0,2:T(4,128)}, u32[]{:S(2)}, u32[]{:S(2)}) %all-to-all-start.3) | async-done | bytes 3932192 | tf_op jit(solution)/shard_map/all_to_all | solution.py:182
  719.0 4.7 copy.289
  723.7 3.9 gather_fusion.3
  727.6 4.6 bitcast_select_fusion.2
  (154 shorter events, 58.3 us)
Async XLA Ops:
  0.6 13.0 %copy-start = (f32[5,4,48,384]{3,2,1,0:T(8,128)S(1)}, f32[5,4,48,384]{3,2,1,0:T(8,128)}, u32[]{:S(2)}) copy-start(f32[5,4,48,384]{3,2,1,0:T(8,128)} %param.7) | copy-start | bytes 4423684
  1.9 11.7 %collective-permute-start.4 = (f32[5,4,1,384]{3,1,2,0:T(4,128)S(1)}, f32[5,4,1,384]{3,1,2,0:T(4,128)S(1)}, u32[]{:S(2)}, u32[]{:S(2)}) collective-permute-start(f32[5,4,1,384]{3,1,2,0:T(4,128)S(1)} %copy.294), channel_id=1, source_target_pairs={{0,16},{16,32},{32,48},{48,64},{64,80},{80,96},{96,112},{1,17},{17... | collective-permute-start | bytes 92168 | tf_op jit(solution)/shard_map/ppermute | solution.py:21
  6.4 7.2 collective-permute-start.5
  13.6 9.7 %copy-start.10 = (f32[5,4,1,384]{3,2,1,0:T(1,128)}, f32[5,4,1,384]{3,2,1,0:T(1,128)S(1)}, u32[]{:S(2)}) copy-start(f32[5,4,1,384]{3,2,1,0:T(1,128)S(1)} %copy.248) | copy-start | bytes 92164
  13.7 0.6 copy-start.12
  14.3 6.1 collective-permute-start.6
  17.7 4.4 collective-permute-start.7
  20.7 6.0 copy-start.5
  26.7 3.1 copy-start.19
  29.8 32.2 %copy-start.20 = (pred[2080]{0:T(1024)(128)(4,1)S(1)}, pred[2080]{0:T(1024)(128)(4,1)}, u32[]{:S(2)}) copy-start(pred[2080]{0:T(1024)(128)(4,1)} %reshape.324) | copy-start | bytes 6244
  29.8 32.2 %copy-start.21 = (pred[2080]{0:T(1024)(128)(4,1)S(1)}, pred[2080]{0:T(1024)(128)(4,1)}, u32[]{:S(2)}) copy-start(pred[2080]{0:T(1024)(128)(4,1)} %compare_and_fusion) | copy-start | bytes 6244
  103.2 131.5 %all-to-all-start = ((f32[16,1,124800]{2,1,0:T(1,128)}), f32[16,1,124800]{2,1,0:T(1,128)}, u32[]{:S(2)}, u32[]{:S(2)}) async-start(f32[16,1,124800]{2,1,0:T(1,128)} %reshape.359), calls=%async_computation | async-start | bytes 15974400 | tf_op jit(solution)/shard_map/all_to_all | solution.py:147
  310.5 11.1 %copy-start.9 = (f32[2,4,48,384]{3,2,1,0:T(8,128)S(1)}, f32[2,4,48,384]{3,2,1,0:T(8,128)}, u32[]{:S(2)}) copy-start(f32[2,4,48,384]{3,2,1,0:T(8,128)} %param.11) | copy-start | bytes 1769476
  310.5 49.5 %all-to-all-start.1 = ((f32[5,4,144,130]{3,1,0,2:T(4,128)}), f32[5,4,144,130]{3,1,0,2:T(4,128)S(1)}, u32[]{:S(2)}, u32[]{:S(2)}) async-start(f32[5,4,144,130]{3,1,0,2:T(4,128)} %select_bitcast_fusion.2), calls=%async_computation.1 | async-start | bytes 5898240 | tf_op jit(solution)/shard_map/all_to_all | solution.py:152
  314.8 34.8 %copy-start.3 = (f32[5,4,48,384]{3,2,1,0:T(8,128)S(1)}, f32[5,4,48,384]{3,2,1,0:T(8,128)}, u32[]{:S(2)}) copy-start(f32[5,4,48,384]{3,2,1,0:T(8,128)} %param.10) | copy-start | bytes 4423684
  316.1 31.5 %collective-permute-start = (f32[5,4,1,384]{3,1,2,0:T(4,128)S(1)}, f32[5,4,1,384]{3,1,2,0:T(4,128)S(1)}, u32[]{:S(2)}, u32[]{:S(2)}) collective-permute-start(f32[5,4,1,384]{3,1,2,0:T(4,128)S(1)} %copy.292), channel_id=1, source_target_pairs={{0,16},{16,32},{32,48},{48,64},{64,80},{80,96},{96,112},{1,17},{17... | collective-permute-start | bytes 92168 | tf_op jit(solution)/shard_map/ppermute | solution.py:21
  319.7 30.0 %collective-permute-start.1 = (f32[5,4,1,384]{3,1,2,0:T(4,128)S(1)}, f32[5,4,1,384]{3,1,2,0:T(4,128)S(1)}, u32[]{:S(2)}, u32[]{:S(2)}) collective-permute-start(f32[5,4,1,384]{3,1,2,0:T(4,128)S(1)} %copy.293), channel_id=1, source_target_pairs={{16,0},{32,16},{48,32},{64,48},{80,64},{96,80},{112,96},{17,1},{33... | collective-permute-start | bytes 92168 | tf_op jit(solution)/shard_map/ppermute | solution.py:23
  347.7 3.1 copy-start.13
  349.7 1.1 copy-start.14
  352.1 4.2 collective-permute-start.2
  354.2 4.6 collective-permute-start.3
  365.8 3.6 copy-start.4
  365.8 3.6 copy-start.7
  365.8 3.6 copy-start.8
  373.0 9.2 %copy-start.2 = (f32[5,4,48,384]{3,2,1,0:T(8,128)}, f32[5,4,48,384]{3,2,1,0:T(8,128)S(1)}, u32[]{:S(2)}) copy-start(f32[5,4,48,384]{3,2,1,0:T(8,128)S(1)} %multiply_add_fusion.2) | copy-start | bytes 4423684
  373.1 5.5 collective-permute-start.8
  376.6 5.2 collective-permute-start.9
  378.6 3.8 copy-start.16
  381.9 0.6 copy-start.18
  382.5 3.9 collective-permute-start.10
  384.4 4.4 collective-permute-start.11
  395.7 5.8 collective-permute-start.12
  399.0 5.2 collective-permute-start.13
  401.5 2.8 copy-start.15
  404.3 1.3 copy-start.17
  406.9 9.9 %collective-permute-start.14 = (f32[5,4,50,1]{2,1,3,0:T(4,128)S(1)}, f32[5,4,50,1]{2,1,3,0:T(4,128)}, u32[]{:S(2)}, u32[]{:S(2)}) collective-permute-start(f32[5,4,50,1]{2,1,3,0:T(4,128)S(1)} %copy.281), channel_id=1, source_target_pairs={{0,1},{1,2},{2,3},{3,4},{4,5},{5,6},{6,7},{7,8},{8,9},{9,10},{10,1... | collective-permute-start | bytes 12008 | tf_op jit(solution)/shard_map/ppermute | solution.py:21
  414.9 4.7 collective-permute-start.15
  541.3 50.2 %all-to-all-start.2 = ((f32[16,1,40960]{2,1,0:T(1,128)}), f32[16,1,40960]{2,1,0:T(1,128)S(1)}, u32[]{:S(2)}, u32[]{:S(2)}) async-start(f32[16,1,40960]{2,1,0:T(1,128)} %reshape.361), calls=%async_computation.2 | async-start | bytes 5242880 | tf_op jit(solution)/shard_map/all_to_all | solution.py:179
  667.6 51.4 %all-to-all-start.3 = ((f32[5,4,128,384]{3,1,0,2:T(4,128)}), f32[5,4,128,384]{3,1,0,2:T(4,128)}, u32[]{:S(2)}, u32[]{:S(2)}) async-start(f32[5,4,128,384]{3,1,0,2:T(4,128)} %bitcast_select_fusion.1), calls=%async_computation.3 | async-start | bytes 7864320 | tf_op jit(solution)/shard_map/all_to_all | solution.py:182
  674.8 0.6 copy-start.22
  723.7 3.9 copy-start.1
  723.7 3.9 copy-start.6
  723.7 3.9 copy-start.11
where the time goes:
time: 743 us; the launch traced here: 733 us
  local copies, waits for them, and re-layouts  276 us (37%)
  waiting for transfers between devices  241 us (32%)
  other arithmetic  144 us (19%)
  starting transfers between devices  67.1 us (9%)
    all_to_all x2, waiting for transfers between devices, per_device(): lax.all_to_all(outgoing, 'gy', split_axis=3, concat_axis=3, tiled=True)  160 us
    unnamed x54, local copies, waits for them, and re-layouts  102 us
    reshape x1, local copies, waits for them, and re-layouts, block_mean(): state.reshape(extent[0], extent[1], extent[2] // 3, 3, extent[3] // 3, 3)  61.8 us
    gather x2, local copies, waits for them, and re-layouts, take_columns(): jnp.take(values, jnp.clip(positions, 0, values.shape[3] - 1), axis=3)  44.5 us
    all_to_all x2, waiting for transfers between devices, per_device(): lax.all_to_all(outgoing_rows, 'gx', split_axis=2, concat_axis=2, tiled=True)  42.9 us
    all_to_all x2, other arithmetic, per_device(): lax.all_to_all(outgoing, 'gy', split_axis=3, concat_axis=3, tiled=True)  33.8 us
    ppermute x8, starting transfers between devices, extended(): lax.ppermute(tail, axis, [(i, (i + 1) % count) for i in range(ends)])  27.1 us
    ppermute x8, waiting for transfers between devices, extended(): lax.ppermute(tail, axis, [(i, (i + 1) % count) for i in range(ends)])  24.9 us
  transfers between devices with their start and end apart: 20, of which 11 were waited for; matrix products, arithmetic and copies ran while one was open for 4% of the time, Pallas kernels for 0%

commit v1 on v0

--- a/solution.py
+++ b/solution.py
@@ -176,7 +176,10 @@
     rows_valid = within(relative_rows, row_devices * span_rows)
     columns_valid = within(relative_columns, column_devices * span_columns)
     outgoing = spread_columns(coarse, own_columns // parent_columns, column_devices)
-    incoming = lax.all_to_all(outgoing, "gy", split_axis=3, concat_axis=3, tiled=True)
+    incoming = jnp.concatenate(
+        lax.all_to_all(jnp.stack(jnp.split(outgoing, lax.axis_size("gy"), axis=3)), "gy", 0, 0),
+        axis=3,
+    )
     placed = take_columns(incoming, relative_columns, columns_valid)
     outgoing_rows = spread_rows(placed, own_rows // parent_rows, row_devices)
     incoming_rows = lax.all_to_all(outgoing_rows, "gx", split_axis=2, concat_axis=2, tiled=True)

time: 743 us -> 707 us (0.952)
  local copies, waits for them, and re-layouts: 276 us -> 248 us
    all_to_all x0 -> x1, waiting for transfers between devices: none -> 40.5 us  [per_device(): lax.all_to_all(jnp.stack(jnp.split(outgoing, lax.axis_size('gy'), axis=3)...]
    all_to_all x2 -> x1, waiting for transfers between devices: 160 us -> 120 us  [per_device(): lax.all_to_all(outgoing, 'gy', split_axis=3, concat_axis=3, tiled=True)]
    unnamed x54 -> x53, local copies, waits for them, and re-layouts: 102 us -> 65.2 us
    all_to_all x2 -> x1, local copies, waits for them, and re-layouts: 17.7 us -> 0.51 us  [per_device(): lax.all_to_all(outgoing, 'gy', split_axis=3, concat_axis=3, tiled=True)]
    reshape x0 -> x1, local copies, waits for them, and re-layouts: none -> 14.8 us  [per_device(): jnp.concatenate(lax.all_to_all(jnp.stack(jnp.split(outgoing, lax.axis_siz...]
    select_n x1, other arithmetic: 11.5 us -> 1.94 us  [spread_columns(): return jnp.where(owner_mask(owners, count), tiled, 0.0)]
    all_to_all x2 -> x1, other arithmetic: 33.8 us -> 24.7 us  [per_device(): lax.all_to_all(outgoing, 'gy', split_axis=3, concat_axis=3, tiled=True)]
    all_to_all x0 -> x1, starting transfers between devices: none -> 8.93 us  [per_device(): lax.all_to_all(jnp.stack(jnp.split(outgoing, lax.axis_size('gy'), axis=3)...]
  transfers between devices with their start and end apart: 20 -> 20, of which waited for: 11 -> 11; matrix products, arithmetic and copies ran while one was open for 4% -> 5% of each run, Pallas kernels for 0% -> 0%
where the time goes in v1:
time: 707 us; the launch traced here: 696 us
  local copies, waits for them, and re-layouts  248 us (35%)
  waiting for transfers between devices  239 us (34%)
  other arithmetic  137 us (19%)
  starting transfers between devices  68.8 us (10%)
    all_to_all x1, waiting for transfers between devices, per_device(): lax.all_to_all(outgoing, 'gy', split_axis=3, concat_axis=3, tiled=True)  120 us
    unnamed x53, local copies, waits for them, and re-layouts  65.2 us
    reshape x1, local copies, waits for them, and re-layouts, block_mean(): state.reshape(extent[0], extent[1], extent[2] // 3, 3, extent[3] // 3, 3)  61.7 us
    gather x2, local copies, waits for them, and re-layouts, take_columns(): jnp.take(values, jnp.clip(positions, 0, values.shape[3] - 1), axis=3)  44.7 us
    all_to_all x2, waiting for transfers between devices, per_device(): lax.all_to_all(outgoing_rows, 'gx', split_axis=2, concat_axis=2, tiled=True)  42.9 us
    all_to_all x1, waiting for transfers between devices, per_device(): lax.all_to_all(jnp.stack(jnp.split(outgoing, lax.axis_size('gy'), axis=3)...  40.5 us
    ppermute x8, starting transfers between devices, extended(): lax.ppermute(tail, axis, [(i, (i + 1) % count) for i in range(ends)])  27 us
    all_to_all x1, other arithmetic, per_device(): lax.all_to_all(outgoing, 'gy', split_axis=3, concat_axis=3, tiled=True)  24.7 us
  transfers between devices with their start and end apart: 20, of which 11 were waited for; matrix products, arithmetic and copies ran while one was open for 5% of the time, Pallas kernels for 0%

profile of v1, /device:TPU:1, one launch (start us, length us, event | category | flops | bytes accessed | tf_op | source)
XLA Modules:
  0.0 696.4 jit_solution(14712670385526613144)
XLA Ops:
  1.9 4.5 collective-permute-start.4
  10.6 2.1 maximum_bitcast_fusion.1
  14.1 3.2 collective-permute-start.6
  23.1 3.4 fusion.34
  26.5 3.1 copy.273
  29.5 32.3 %gather_fusion = f32[2080,5,4,48]{3,2,1,0:T(4,128)} fusion(f32[5,4,48,384]{2,1,3,0:T(4,128)} %copy.273, s32[3072]{0:T(1024)} %pad_clamp_fusion), kind=kCustom, calls=%fused_computation | custom fusion | bytes 15982720 | tf_op jit(solution)/shard_map/jit(_take)/gather | solution.py:87
  61.9 15.2 %fusion.103 = f32[2080,5,4,48]{3,2,1,0:T(4,128)} fusion(f32[2080,5,4,48]{3,2,1,0:T(4,128)} %gather_fusion, pred[2080]{0:T(1024)(128)(4,1)S(1)} %copy-done.12, pred[2080]{0:T(1024)(128)(4,1)S(1)} %copy-done.11), kind=kLoop, calls=%fused_computation.227 | loop fusion | flops 3993600 | bytes 15978560
  77.0 26.0 %reshape.367 = f32[16,1,124800]{2,1,0:T(1,128)} reshape(f32[2080,5,4,48]{3,2,1,0:T(4,128)} %fusion.103) | data formatting | bytes 15974400
  103.0 9.8 %all-to-all-start = ((f32[16,1,124800]{2,1,0:T(1,128)}), f32[16,1,124800]{2,1,0:T(1,128)}, u32[]{:S(2)}, u32[]{:S(2)}) async-start(f32[16,1,124800]{2,1,0:T(1,128)} %reshape.367), calls=%async_computation | async-start | bytes 15974400 | tf_op jit(solution)/shard_map/all_to_all | solution.py:147
  115.0 119.8 %all-to-all-done = f32[16,1,124800]{2,1,0:T(1,128)} async-done(((f32[16,1,124800]{2,1,0:T(1,128)}), f32[16,1,124800]{2,1,0:T(1,128)}, u32[]{:S(2)}, u32[]{:S(2)}) %all-to-all-start) | async-done | bytes 7987232 | tf_op jit(solution)/shard_map/all_to_all | solution.py:147
  235.3 24.7 %reduce.4 = f32[16,124800]{1,0:T(8,128)} reduce(f32[16,1,124800]{2,1,0:T(1,128)} %all-to-all-done, f32[]{:T(128)} %broadcast.601), dimensions={1}, to_apply=%all_to_all.12.reduce_sub_computation | reduce | bytes 15974404 | tf_op jit(solution)/shard_map/all_to_all | solution.py:147
  260.0 28.8 %reshape.368 = f32[2080,5,4,48]{3,2,1,0:T(4,128)} reshape(f32[16,124800]{1,0:T(8,128)} %reduce.4) | data formatting | bytes 15974400
  288.8 12.9 %reduce_sum.27 = f32[5,4,48,130]{2,1,0,3:T(4,128)} reduce(f32[5,4,48,16,130]{2,1,0,4,3:T(4,128)} %bitcast.124, f32[]{:T(128)} %constant.66.clone.1), dimensions={3}, to_apply=%region_0.1 | reduce | flops 1872000 | bytes 8486404 | tf_op jit(solution)/shard_map/reduce_sum | solution.py:150
  301.7 2.4 copy.274
  304.1 4.3 gather_fusion.1
  308.5 3.9 select_bitcast_fusion.2
  312.4 5.1 all-to-all-start.1
  317.6 3.5 collective-permute-start
  323.7 2.1 maximum_bitcast_fusion.3
  326.3 24.0 %collective-permute-done = f32[5,4,1,384]{3,1,2,0:T(4,128)S(1)} collective-permute-done((f32[5,4,1,384]{3,1,2,0:T(4,128)S(1)}, f32[5,4,1,384]{3,1,2,0:T(4,128)S(1)}, u32[]{:S(2)}, u32[]{:S(2)}) %collective-permute-start) | collective-permute-done | bytes 30752 | tf_op jit(solution)/shard_map/ppermute | solution.py:21
  350.3 2.1 collective-permute-done.1
  363.2 2.5 reduce_sum.28
  367.2 3.5 copy.278
  370.8 3.4 copy.279
  374.2 5.7 multiply_add_fusion.2
  379.9 3.4 collective-permute-start.8
  385.4 3.2 collective-permute-done.9
  391.8 3.1 collective-permute-start.10
  403.3 5.6 multiply_add_fusion.1
  409.0 3.3 collective-permute-start.12
  414.9 2.7 collective-permute-done.13
  420.8 4.6 collective-permute-start.14
  433.9 6.6 multiply_add_fusion
  440.5 61.7 %reshape.328 = f32[5,4,16,3,128,3]{5,4,3,2,1,0:T(8,128)} reshape(f32[5,4,48,384]{3,2,1,0:T(8,128)} %multiply_add_fusion) | data formatting | bytes 2949120 | tf_op jit(solution)/shard_map/reshape | solution.py:70
  502.2 20.5 %reduce_sum.29 = f32[5,4,16,128]{3,2,1,0:T(8,128)S(1)} reduce(f32[5,4,16,3,128,3]{5,4,3,2,1,0:T(8,128)} %reshape.328, f32[]{:T(128)} %constant.66.clone.1), dimensions={3,5}, to_apply=%region_2.3 | reduce | flops 327680 | bytes 1638404 | tf_op jit(solution)/shard_map/reduce_sum | solution.py:71
  524.4 3.7 tile.9
  541.1 8.9 %all-to-all-start.2 = ((f32[16,5,4,16,128]{4,3,2,1,0:T(8,128)}), f32[16,5,4,16,128]{4,3,2,1,0:T(8,128)}, u32[]{:S(2)}, u32[]{:S(2)}) async-start(f32[16,5,4,16,128]{4,3,2,1,0:T(8,128)} %fusion.65), calls=%async_computation.2 | async-start | bytes 5242880 | tf_op jit(solution)/shard_map/all_to_all | solution.py:180
  551.9 40.5 %all-to-all-done.2 = f32[16,5,4,16,128]{4,3,2,1,0:T(8,128)} async-done(((f32[16,5,4,16,128]{4,3,2,1,0:T(8,128)}), f32[16,5,4,16,128]{4,3,2,1,0:T(8,128)}, u32[]{:S(2)}, u32[]{:S(2)}) %all-to-all-start.2) | async-done | bytes 2621472 | tf_op jit(solution)/shard_map/all_to_all | solution.py:180
  592.4 14.8 %copy.308 = f32[5,4,16,16,128]{2,1,4,3,0:T(4,128)} copy(f32[5,4,16,16,128]{4,2,1,0,3:T(8,128)} %bitcast.40) | data formatting | bytes 5242880 | tf_op jit(solution)/shard_map/reshape | solution.py:179
  607.2 12.3 %gather_fusion.2 = f32[384,5,4,16]{3,2,1,0:T(4,128)} fusion(f32[5,4,16,2048]{2,1,3,0:T(4,128)} %bitcast.125, s32[1024]{0:T(1024)S(1)} %copy-done.13), kind=kCustom, calls=%fused_computation.2 | custom fusion | bytes 984576 | tf_op jit(solution)/shard_map/jit(_take)/gather | solution.py:87
  619.6 6.0 select_bitcast_fusion.1
  625.6 3.4 copy.304
  628.9 2.8 bitcast_select_fusion
  631.8 5.2 all-to-all-start.3
  640.1 42.9 %all-to-all-done.3 = f32[5,4,128,384]{3,1,0,2:T(4,128)} async-done(((f32[5,4,128,384]{3,1,0,2:T(4,128)}), f32[5,4,128,384]{3,1,0,2:T(4,128)}, u32[]{:S(2)}, u32[]{:S(2)}) %all-to-all-start.3) | async-done | bytes 3932192 | tf_op jit(solution)/shard_map/all_to_all | solution.py:185
  683.0 4.7 copy.305
  687.7 3.8 gather_fusion.3
  691.5 4.6 bitcast_select_fusion.1
  (153 shorter events, 75.9 us)
Async XLA Ops:
  0.6 12.9 %copy-start = (f32[5,4,48,384]{3,2,1,0:T(8,128)S(1)}, f32[5,4,48,384]{3,2,1,0:T(8,128)}, u32[]{:S(2)}) copy-start(f32[5,4,48,384]{3,2,1,0:T(8,128)} %param.7) | copy-start | bytes 4423684
  1.9 11.5 %collective-permute-start.4 = (f32[5,4,1,384]{3,1,2,0:T(4,128)S(1)}, f32[5,4,1,384]{3,1,2,0:T(4,128)S(1)}, u32[]{:S(2)}, u32[]{:S(2)}) collective-permute-start(f32[5,4,1,384]{3,1,2,0:T(4,128)S(1)} %copy.312), channel_id=1, source_target_pairs={{0,16},{16,32},{32,48},{48,64},{64,80},{80,96},{96,112},{1,17},{17... | collective-permute-start | bytes 92168 | tf_op jit(solution)/shard_map/ppermute | solution.py:21
  6.4 7.0 %collective-permute-start.5 = (f32[5,4,1,384]{3,1,2,0:T(4,128)S(1)}, f32[5,4,1,384]{3,1,2,0:T(4,128)S(1)}, u32[]{:S(2)}, u32[]{:S(2)}) collective-permute-start(f32[5,4,1,384]{3,1,2,0:T(4,128)S(1)} %copy.313), channel_id=1, source_target_pairs={{16,0},{32,16},{48,32},{64,48},{80,64},{96,80},{112,96},{17,1},{33... | collective-permute-start | bytes 92168 | tf_op jit(solution)/shard_map/ppermute | solution.py:23
  13.5 0.6 copy-start.4
  14.1 6.1 collective-permute-start.6
  17.6 4.4 collective-permute-start.7
  29.5 32.3 %copy-start.11 = (pred[2080]{0:T(1024)(128)(4,1)S(1)}, pred[2080]{0:T(1024)(128)(4,1)}, u32[]{:S(2)}) copy-start(pred[2080]{0:T(1024)(128)(4,1)} %reshape.332) | copy-start | bytes 6244
  29.5 32.3 %copy-start.12 = (pred[2080]{0:T(1024)(128)(4,1)S(1)}, pred[2080]{0:T(1024)(128)(4,1)}, u32[]{:S(2)}) copy-start(pred[2080]{0:T(1024)(128)(4,1)} %compare_and_fusion) | copy-start | bytes 6244
  103.0 131.8 %all-to-all-start = ((f32[16,1,124800]{2,1,0:T(1,128)}), f32[16,1,124800]{2,1,0:T(1,128)}, u32[]{:S(2)}, u32[]{:S(2)}) async-start(f32[16,1,124800]{2,1,0:T(1,128)} %reshape.367), calls=%async_computation | async-start | bytes 15974400 | tf_op jit(solution)/shard_map/all_to_all | solution.py:147
  312.4 5.1 copy-start.3
  312.4 50.8 %all-to-all-start.1 = ((f32[5,4,144,130]{3,1,0,2:T(4,128)}), f32[5,4,144,130]{3,1,0,2:T(4,128)}, u32[]{:S(2)}, u32[]{:S(2)}) async-start(f32[5,4,144,130]{3,1,0,2:T(4,128)} %select_bitcast_fusion.2), calls=%async_computation.1 | async-start | bytes 5898240 | tf_op jit(solution)/shard_map/all_to_all | solution.py:152
  317.6 32.7 %collective-permute-start = (f32[5,4,1,384]{3,1,2,0:T(4,128)S(1)}, f32[5,4,1,384]{3,1,2,0:T(4,128)S(1)}, u32[]{:S(2)}, u32[]{:S(2)}) collective-permute-start(f32[5,4,1,384]{3,1,2,0:T(4,128)S(1)} %copy.310), channel_id=1, source_target_pairs={{0,16},{16,32},{32,48},{48,64},{64,80},{80,96},{96,112},{1,17},{17... | collective-permute-start | bytes 92168 | tf_op jit(solution)/shard_map/ppermute | solution.py:21
  321.2 31.2 %collective-permute-start.1 = (f32[5,4,1,384]{3,1,2,0:T(4,128)S(1)}, f32[5,4,1,384]{3,1,2,0:T(4,128)S(1)}, u32[]{:S(2)}, u32[]{:S(2)}) collective-permute-start(f32[5,4,1,384]{3,1,2,0:T(4,128)S(1)} %copy.311), channel_id=1, source_target_pairs={{16,0},{32,16},{48,32},{64,48},{80,64},{96,80},{112,96},{17,1},{33... | collective-permute-start | bytes 92168 | tf_op jit(solution)/shard_map/ppermute | solution.py:23
  350.3 3.4 copy-start.5
  352.4 1.3 copy-start.6
  355.1 5.3 collective-permute-start.2
  357.7 4.4 collective-permute-start.3
  379.9 10.1 %copy-start.2 = (f32[5,4,48,384]{3,2,1,0:T(8,128)}, f32[5,4,48,384]{3,2,1,0:T(8,128)S(1)}, u32[]{:S(2)}) copy-start(f32[5,4,48,384]{3,2,1,0:T(8,128)S(1)} %multiply_add_fusion.2) | copy-start | bytes 4423684
  379.9 5.4 collective-permute-start.8
  383.4 5.2 collective-permute-start.9
  385.4 3.3 copy-start.8
  388.6 1.3 copy-start.10
  391.8 6.8 collective-permute-start.10
  396.8 4.7 collective-permute-start.11
  408.9 10.0 %copy-start.1 = (f32[5,4,48,384]{3,2,1,0:T(8,128)}, f32[5,4,48,384]{3,2,1,0:T(8,128)S(1)}, u32[]{:S(2)}) copy-start(f32[5,4,48,384]{3,2,1,0:T(8,128)S(1)} %multiply_add_fusion.1) | copy-start | bytes 4423684
  409.0 5.9 collective-permute-start.12
  412.4 5.2 collective-permute-start.13
  414.9 2.7 copy-start.7
  417.6 1.3 copy-start.9
  420.8 9.0 %collective-permute-start.14 = (f32[5,4,50,1]{2,1,3,0:T(4,128)}, f32[5,4,50,1]{2,1,3,0:T(4,128)}, u32[]{:S(2)}, u32[]{:S(2)}) collective-permute-start(f32[5,4,50,1]{2,1,3,0:T(4,128)} %copy.297), channel_id=1, source_target_pairs={{0,1},{1,2},{2,3},{3,4},{4,5},{5,6},{6,7},{7,8},{8,9},{9,10},{10,1... | collective-permute-start | bytes 12008 | tf_op jit(solution)/shard_map/ppermute | solution.py:21
  427.3 4.7 collective-permute-start.15
  524.4 3.7 copy-start.14
  541.1 51.3 %all-to-all-start.2 = ((f32[16,5,4,16,128]{4,3,2,1,0:T(8,128)}), f32[16,5,4,16,128]{4,3,2,1,0:T(8,128)}, u32[]{:S(2)}, u32[]{:S(2)}) async-start(f32[16,5,4,16,128]{4,3,2,1,0:T(8,128)} %fusion.65), calls=%async_computation.2 | async-start | bytes 5242880 | tf_op jit(solution)/shard_map/all_to_all | solution.py:180
  592.4 14.8 %copy-start.13 = (s32[1024]{0:T(1024)S(1)}, s32[1024]{0:T(1024)}, u32[]{:S(2)}) copy-start(s32[1024]{0:T(1024)} %get-tuple-element.40) | copy-start | bytes 12292
  631.8 51.2 %all-to-all-start.3 = ((f32[5,4,128,384]{3,1,0,2:T(4,128)}), f32[5,4,128,384]{3,1,0,2:T(4,128)}, u32[]{:S(2)}, u32[]{:S(2)}) async-start(f32[5,4,128,384]{3,1,0,2:T(4,128)} %bitcast_select_fusion), calls=%async_computation.3 | async-start | bytes 7864320 | tf_op jit(solution)/shard_map/all_to_all | solution.py:185
  638.8 0.6 copy-start.15
